TPU v7x, 32 devices: a whole 2x2x4 slice. The times are simulated.
32 devices in a mesh: row: 8 (over y, x, core), col: 4 (over z).
Axes of the slice: x: 2, y: 2, z: 4, core: 2. Of those that a mesh axis runs over, the one named last changes fastest.
Arguments:
- pair: bfloat16 [256, 256, 128], P('row', 'col'), may hold values from -6 to 6
- cotangent: bfloat16 [256, 256, 128], P('row', 'col'), may hold values from -6 to 6
- length: int32 [1], replicated, may hold values from 128 to 256
- norm_gain: float32 [128], replicated, may hold values from 0.1 to 1.9
- norm_bias: float32 [128], replicated, may hold values from -1.5 to 1.5
- left_weight: bfloat16 [128, 256], replicated, may hold values from -0.5 to 0.5
- right_weight: bfloat16 [128, 256], replicated, may hold values from -0.5 to 0.5
- gate_weight: bfloat16 [128, 128], replicated, may hold values from -0.5 to 0.5
- out_gain: float32 [128], replicated, may hold values from 0.1 to 1.9
- out_bias: float32 [128], replicated, may hold values from -2 to 2
- out_weight: bfloat16 [128, 128], replicated, may hold values from -0.5 to 0.5
Outputs:
- update: bfloat16 [256, 256, 128], P('row', 'col')
- grad_pair: bfloat16 [256, 256, 128], P('row', 'col')
- grad_left: float32 [128, 256], replicated
- grad_right: float32 [128, 256], replicated
- grad_gating: float32 [128, 128], replicated
- grad_output: float32 [128, 128], replicated
- grad_norms: float32 [4, 128], replicated
Inputs may be any that keep to these rules, and one draw needn't show every extreme that they name: Tokens at positions 255 down to length are padding.
All inputs are finite; a program needn't handle non-finite values.
Results may differ from a plain program's by a relative error of at most 0.014.
Values may be sent and summed in bfloat16 or wider, within the bound.
No kernel may reach another device: no remote copies, remote signals or barrier semaphores. Data moves between devices by JAX's collectives and lax.ppermute only.
A program may use at most 128 MiB of HBM per device.

v0:
```python
import jax
import jax.numpy as jnp
from jax import lax
from jax.sharding import PartitionSpec as P

EPS = 1e-05


def broadcast(block, axis, holder):
    block = jnp.where(lax.axis_index(axis) == holder, block, jnp.zeros_like(block))
    return lax.psum(block, axis)


def normalize(values):
    center = values - jnp.mean(values, axis=-1, keepdims=True)
    inverse = lax.rsqrt(jnp.mean(center * center, axis=-1, keepdims=True) + EPS)
    return (center * inverse, inverse)


def gating(panel, weight, first_ok, second_ok, hidden):
    projected = jnp.einsum("ikc,ch->ikh", panel, weight, preferred_element_type=jnp.float32)
    values = projected[..., :hidden]
    sigmoid_val = jax.nn.sigmoid(projected[..., hidden:])
    pad_mask = (first_ok[:, None] & second_ok[None, :]).astype(jnp.float32)[..., None]
    return ((pad_mask * sigmoid_val * values).astype(jnp.bfloat16), values, sigmoid_val, pad_mask)


def push_back(partial_value, values, sigmoid_val, pad_mask, weight, panel):
    combined = jnp.concatenate(
        [
            partial_value * pad_mask * sigmoid_val,
            partial_value * pad_mask * values * sigmoid_val * (1.0 - sigmoid_val),
        ],
        axis=-1,
    ).astype(jnp.bfloat16)
    panel_grad = jnp.einsum("ikh,ch->ikc", combined, weight, preferred_element_type=jnp.float32)
    weight_grad = jnp.einsum("ikc,ikh->ch", panel, combined, preferred_element_type=jnp.float32)
    return (panel_grad, weight_grad)


def per_device(
    pair,
    cotangent,
    length,
    norm_gain,
    norm_bias,
    left_weight,
    right_weight,
    gate_weight,
    out_gain,
    out_bias,
    out_weight,
):
    row_index = lax.axis_index("row")
    col_index = lax.axis_index("col")
    n_row = lax.axis_size("row")
    n_col = lax.axis_size("col")
    per_col = n_row // n_col
    rows_dev = pair.shape[0]
    cols_dev = pair.shape[1]
    tokens = rows_dev * n_row
    hidden = out_weight.shape[0]
    pair_hat, pair_scale = normalize(pair.astype(jnp.float32))
    normed = (pair_hat * norm_gain + norm_bias).astype(jnp.bfloat16)
    real_count = length[0]
    second_ok = jnp.arange(tokens, dtype=jnp.int32) < real_count
    own_ok = row_index * rows_dev + jnp.arange(rows_dev, dtype=jnp.int32) < real_count
    partner_ok = col_index * cols_dev + jnp.arange(cols_dev, dtype=jnp.int32) < real_count
    left_tile, left_val, left_sig, tile_mask = gating(
        normed, left_weight, own_ok, partner_ok, hidden
    )
    right_tile, right_val, right_sig, unused_mask = gating(
        normed, right_weight, own_ok, partner_ok, hidden
    )
    row_panel = lax.all_gather(normed, "col", axis=1, tiled=True)
    pieces = []
    for member in range(per_col):
        pieces.append(broadcast(row_panel, "row", col_index * per_col + member))
    col_panel = jnp.concatenate(pieces, axis=0)
    left_act = gating(row_panel, left_weight, own_ok, second_ok, hidden)[0]
    right_act = gating(col_panel, right_weight, partner_ok, second_ok, hidden)[0]
    tri = jnp.einsum("ikh,jkh->ijh", left_act, right_act, preferred_element_type=jnp.float32)
    tri_hat, tri_scale = normalize(tri)
    tri_normed = (tri_hat * out_gain + out_bias).astype(jnp.bfloat16)
    outer_val = jnp.einsum(
        "ijh,hc->ijc", tri_normed, out_weight, preferred_element_type=jnp.float32
    )
    gate_val = jax.nn.sigmoid(
        jnp.einsum("ijc,cd->ijd", normed, gate_weight, preferred_element_type=jnp.float32)
    )
    update = (gate_val * outer_val).astype(jnp.bfloat16)
    upstream = cotangent.astype(jnp.float32)
    outer_grad = (upstream * gate_val).astype(jnp.bfloat16)
    gate_grad = (upstream * outer_val * gate_val * (1.0 - gate_val)).astype(jnp.bfloat16)
    grad_output = jnp.einsum(
        "ijh,ijc->hc", tri_normed, outer_grad, preferred_element_type=jnp.float32
    )
    grad_gating = jnp.einsum("ijc,ijd->cd", normed, gate_grad, preferred_element_type=jnp.float32)
    tnorm_grad = jnp.einsum(
        "ijc,hc->ijh", outer_grad, out_weight, preferred_element_type=jnp.float32
    )
    hat_grad = tnorm_grad * out_gain
    tri_grad = (
        tri_scale
        * (
            hat_grad
            - jnp.mean(hat_grad, axis=-1, keepdims=True)
            - tri_hat * jnp.mean(hat_grad * tri_hat, axis=-1, keepdims=True)
        )
    ).astype(jnp.bfloat16)
    row_partial = jnp.einsum(
        "ijh,jkh->ikh", tri_grad, right_act, preferred_element_type=jnp.float32
    )
    col_partial = jnp.einsum("ijh,ikh->jkh", tri_grad, left_act, preferred_element_type=jnp.float32)
    row_part = lax.psum_scatter(
        row_partial.astype(jnp.bfloat16), "col", scatter_dimension=1, tiled=True
    ).astype(jnp.float32)
    summed = lax.psum_scatter(
        col_partial.astype(jnp.bfloat16), "row", scatter_dimension=0, tiled=True
    )
    slab = summed[None]
    received = lax.all_to_all(slab, "col", split_axis=2, concat_axis=0, tiled=True)
    select = (jnp.arange(per_col, dtype=jnp.int32) == row_index // n_col).astype(jnp.bfloat16)
    spread = (received[:, None] * select[None, :, None, None, None]).reshape(
        (n_row,) + received.shape[1:]
    )
    returned = lax.all_to_all(spread, "row", split_axis=0, concat_axis=0, tiled=True)
    start = row_index % per_col * n_col
    owned = lax.dynamic_slice_in_dim(returned, start, n_col, 0).reshape(rows_dev, cols_dev, -1)
    col_part = owned.astype(jnp.float32)
    from_rows, grad_left = push_back(row_part, left_val, left_sig, tile_mask, left_weight, normed)
    from_cols, grad_right = push_back(
        col_part, right_val, right_sig, tile_mask, right_weight, normed
    )
    gate_back = jnp.einsum(
        "ijd,cd->ijc", gate_grad, gate_weight, preferred_element_type=jnp.float32
    )
    normed_grad = gate_back + from_rows + from_cols
    scaled = normed_grad * norm_gain
    grad_pair = (
        pair_scale
        * (
            scaled
            - jnp.mean(scaled, axis=-1, keepdims=True)
            - pair_hat * jnp.mean(scaled * pair_hat, axis=-1, keepdims=True)
        )
    ).astype(jnp.bfloat16)
    grad_norms = jnp.stack(
        [
            jnp.sum(normed_grad * pair_hat, axis=(0, 1)),
            jnp.sum(normed_grad, axis=(0, 1)),
            jnp.sum(tnorm_grad * tri_hat, axis=(0, 1)),
            jnp.sum(tnorm_grad, axis=(0, 1)),
        ]
    )
    totals = lax.psum((grad_left, grad_right, grad_gating, grad_output, grad_norms), ("row", "col"))
    inverse = 1.0 / tokens
    return (
        update,
        grad_pair,
        totals[0] * inverse,
        totals[1] * inverse,
        totals[2] * inverse,
        totals[3] * inverse,
        totals[4] * inverse,
    )


def solution(mesh):
    return jax.shard_map(
        per_device,
        mesh=mesh,
        in_specs=(
            P("row", "col", None),
            P("row", "col", None),
            P(),
            P(),
            P(),
            P(),
            P(),
            P(),
            P(),
            P(),
            P(),
        ),
        out_specs=(P("row", "col", None), P("row", "col", None), P(), P(), P(), P(), P()),
        check_vma=False,
    )
```

profile of v0, /device:TPU:0, one launch (start us, length us, event | category | flops | bytes accessed | tf_op | source)
XLA Modules:
  0.0 473.8 jit_solution(4896643660126480447)
XLA Ops:
  7.2 1.4 convert_reduce_fusion
  8.6 1.7 fusion.31
  10.3 2.5 fusion.25
  12.8 0.0 all-reduce.7.cloned.1.call-start
  12.9 1.5 fusion.17
  14.4 47.0 %all-gather.2.cloned.1.call-done = bf16[32,256,128]{2,1,0:T(8,128)(2,1)} async-done(((bf16[32,64,128]{2,1,0:T(8,128)(2,1)}), bf16[32,256,128]{2,1,0:T(8,128)(2,1)}) %all-gather.2.cloned.1.call-update) | async-done | bytes 2097168 | tf_op jit(solution)/shard_map/all_gather | solution.py:75
  61.4 3.8 broadcast_select_fusion.1
  65.2 0.2 reduce-scatter.7.cloned.1.call-start
  65.5 0.8 copy-done.6
  66.2 1.3 fusion.73
  68.3 3.1 copy.54
  71.4 0.1 and_convert_fusion.1
  71.5 0.1 and_convert_fusion
  71.5 2.8 fusion.53
  74.4 2.7 fusion.5
  77.0 4.6 copy.52
  81.6 63.4 %all-reduce.7.cloned.1.call-done = (bf16[32,256,128]{2,1,0:T(8,128)(2,1)}, bf16[32,256,128]{2,1,0:T(8,128)(2,1)}) async-done(((bf16[32,256,128]{2,1,0:T(8,128)(2,1)}, bf16[32,256,128]{2,1,0:T(8,128)(2,1)}), (bf16[32,256,128]{2,1,0:T(8,128)(2,1)}, bf16[32,256,128]{2,1,0:T(8,128)(2,1)})) %all-reduce.7.cloned.1.call-update) | async-done | bytes 4194320 | tf_op jit(solution)/shard_map/psum | solution.py:11
  145.1 4.5 fusion.10
  149.6 4.3 fusion
  154.0 6.8 %copy.51 = bf16[64,256,128]{1,0,2:T(8,128)(2,1)} copy(bf16[64,256,128]{2,1,0:T(8,128)(2,1)} %fusion) | data formatting | bytes 8388608 | tf_op jit(solution)/shard_map/convert_element_type | solution.py:25
  160.7 4.1 bitcast_reduce_fusion
  164.9 0.3 multiply_reduce_fusion.2
  165.2 0.3 copy-done.14
  165.5 1.3 multiply_reduce_fusion
  166.8 1.8 multiply_convert_fusion
  168.6 1.3 fusion.74
  169.9 2.2 copy.66
  172.2 0.3 reduce-scatter.5.cloned.1.call-start
  172.5 0.9 copy-done.4
  173.4 4.3 fusion.75
  177.7 4.6 copy.56
  182.4 0.1 mul.265
  182.5 41.1 %reduce-scatter.7.cloned.1.call-done = bf16[8,32768]{1,0:T(8,128)(2,1)} async-done(((bf16[64,32768]{1,0:T(8,128)(2,1)}), bf16[8,32768]{1,0:T(8,128)(2,1)}) %reduce-scatter.7.cloned.1.call-update) | async-done | bytes 524304
  223.6 1.2 copy.71
  224.8 0.3 copy.72
  225.1 1.3 copy.58
  226.4 4.6 all-to-all-start
  231.0 0.1 and_convert_fusion.2
  231.1 1.8 fusion.51
  232.9 1.7 fusion.56
  234.6 1.1 copy.53
  235.7 23.9 %all-to-all-done = bf16[1,8,256,128]{3,1,0,2:T(8,128)(2,1)} async-done(((bf16[1,8,256,128]{3,1,0,2:T(8,128)(2,1)}), bf16[1,8,256,128]{3,1,0,2:T(8,128)(2,1)}, u32[]{:S(2)}, u32[]{:S(2)}) %all-to-all-start) | async-done | bytes 524320 | tf_op jit(solution)/shard_map/all_to_all | solution.py:122
  259.6 1.2 copy.60
  260.8 1.1 bitcast_multiply_fusion
  261.9 4.2 all-to-all-start.1
  266.2 1.2 fusion.34
  267.4 1.0 convolution_bitcast_fusion.3
  268.4 1.0 convolution_bitcast_fusion.2
  269.4 0.3 fusion.63
  269.7 11.9 %all-to-all-done.1 = bf16[8,8,64,128]{3,2,1,0:T(8,128)(2,1)} async-done(((bf16[8,8,64,128]{3,2,1,0:T(8,128)(2,1)}), bf16[8,8,64,128]{3,2,1,0:T(8,128)(2,1)}, u32[]{:S(2)}, u32[]{:S(2)}) %all-to-all-start.1) | async-done | bytes 1048608 | tf_op jit(solution)/shard_map/all_to_all | solution.py:127
  281.5 1.1 constant_dynamic-slice_fusion
  282.7 2.8 fusion.49
  285.5 1.0 convolution_bitcast_fusion.1
  286.5 1.4 convolution_add_fusion.1
  287.9 1.0 convolution_bitcast_fusion
  289.0 2.6 fusion.30
  291.6 37.2 %psum.55 = f32[4,128]{1,0:T(4,128)S(1)} all-reduce(f32[4,128]{1,0:T(4,128)S(1)} %pad_maximum_fusion.6), channel_id=1, replica_groups=mesh['row'=8,'col'=4] {'row','col'}, use_global_device_ids=true, to_apply=%region_20.21 | all-reduce | flops 512 | bytes 4096 | tf_op jit(solution)/shard_map/psum | solution.py:156
  328.8 1.9 fusion.29
  330.8 0.6 broadcast_multiply_fusion.10
  331.3 129.8 %all-reduce.5.cloned.1.call-done = (f32[128,256]{1,0:T(8,128)}, f32[128,256]{1,0:T(8,128)}, f32[128,128]{1,0:T(8,128)}, f32[128,128]{1,0:T(8,128)}) async-done(((f32[128,256]{1,0:T(8,128)}, f32[128,256]{1,0:T(8,128)}, f32[128,128]{1,0:T(8,128)}, f32[128,128]{1,0:T(8,128)}), (f32[128,256]{1,0:T(8,128)}, f32[128,256]{1,0:T(8,128)}, f32[128,128]{1,0:T(8,128)}, ...) | async-done | bytes 393232 | tf_op jit(solution)/shard_map/psum | solution.py:156
  461.2 1.6 broadcast_multiply_fusion
  462.7 1.6 broadcast_multiply_fusion.1
  464.3 1.5 broadcast_multiply_fusion.2
  465.8 1.5 broadcast_multiply_fusion.3
  (50 shorter events, 0.3 us)
Async XLA Ops:
  7.2 137.9 %copy-start = (bf16[128,256]{1,0:T(8,128)(2,1)S(1)}, bf16[128,256]{1,0:T(8,128)(2,1)}, u32[]{:S(2)}) copy-start(bf16[128,256]{1,0:T(8,128)(2,1)} %param.17) | copy-start | bytes 196612
  7.2 5.7 %copy-start.12 = (bf16[128,128]{1,0:T(8,128)(2,1)S(1)}, bf16[128,128]{1,0:T(8,128)(2,1)}, u32[]{:S(2)}) copy-start(bf16[128,128]{1,0:T(8,128)(2,1)} %param.18) | copy-start | bytes 98308
  7.2 54.2 %all-gather.2.cloned.1.call-start = ((), (), s32[]{:S(2)}) async-start(), calls=%async_computation.4 | async-start | bytes 2621440 | tf_op jit(solution)/shard_map/all_gather | solution.py:75
  12.8 132.2 %all-reduce.7.cloned.1.call-start = ((), (), s32[]{:S(2)}) async-start(), calls=%async_computation.8 | async-start | bytes 8388608 | tf_op jit(solution)/shard_map/psum | solution.py:11
  65.2 1.0 copy-start.6
  65.2 1.0 copy-start.11
  65.2 158.4 %reduce-scatter.7.cloned.1.call-start = ((), (), s32[]{:S(2)}) async-start(), calls=%async_computation.6 | async-start | bytes 4718592
  67.6 4.0 copy-start.9
  164.8 0.7 copy-start.14
  165.5 1.3 copy-start.15
  166.8 1.8 copy-start.1
  168.6 1.3 copy-start.3
  172.2 1.2 copy-start.4
  172.2 110.4 %reduce-scatter.5.cloned.1.call-start = ((), (), s32[]{:S(2)}) async-start(), calls=%async_computation.5 | async-start | bytes 2621440 | tf_op jit(solution)/shard_map/reduce_scatter | solution.py:115
  223.6 7.5 %copy-start.2 = (bf16[32,64,128]{2,1,0:T(8,128)(2,1)S(1)}, bf16[32,64,128]{2,1,0:T(8,128)(2,1)}, u32[]{:S(2)}) copy-start(bf16[32,64,128]{2,1,0:T(8,128)(2,1)} %fusion.25) | copy-start | bytes 1572868
  226.4 33.2 %all-to-all-start = ((bf16[1,8,256,128]{3,1,0,2:T(8,128)(2,1)}), bf16[1,8,256,128]{3,1,0,2:T(8,128)(2,1)}, u32[]{:S(2)}, u32[]{:S(2)}) async-start(bf16[1,8,256,128]{3,1,0,2:T(8,128)(2,1)} %copy.58), calls=%async_computation.1 | async-start | bytes 1048576 | tf_op jit(solution)/shard_map/all_to_all | solution.py:122
  231.1 3.5 copy-start.8
  260.8 5.4 %copy-start.7 = (bf16[32,64,128]{2,1,0:T(8,128)(2,1)S(1)}, bf16[32,64,128]{2,1,0:T(8,128)(2,1)}, u32[]{:S(2)}) copy-start(bf16[32,64,128]{2,1,0:T(8,128)(2,1)} %param.12) | copy-start | bytes 1572868
  261.9 19.6 %all-to-all-start.1 = ((bf16[8,8,64,128]{3,2,1,0:T(8,128)(2,1)}), bf16[8,8,64,128]{3,2,1,0:T(8,128)(2,1)}, u32[]{:S(2)}, u32[]{:S(2)}) async-start(bf16[8,8,64,128]{3,2,1,0:T(8,128)(2,1)} %bitcast_multiply_fusion), calls=%async_computation.2 | async-start | bytes 2097152 | tf_op jit(solution)/shard_map/all_to_all | solution.py:127
  266.2 195.0 %all-reduce.5.cloned.1.call-start = ((), (), s32[]{:S(2)}) async-start(), calls=%async_computation.7 | async-start | bytes 786432 | tf_op jit(solution)/shard_map/psum | solution.py:156
  285.5 2.5 copy-start.10
  286.5 2.5 copy-start.5
  286.5 2.5 copy-start.13
Sparse Core Ops, SparseCore 0:
  13.0 48.3 all-gather.1
  65.4 79.6 all-reduce.6
  172.3 51.2 reduce-scatter.6
  225.7 51.5 reduce-scatter.4
  330.9 130.2 all-reduce.4
where the time goes:
time: 475 us; the launch traced here: 474 us
  waiting for transfers between devices  317 us (67%)
  blocking collectives  37.2 us (8%)
  matrix products  32.8 us (7%)
  other arithmetic  32.6 us (7%)
  local copies, waits for them, and re-layouts  29.7 us (6%)
  between operations  14.8 us (3%)
  starting transfers between devices  9.43 us (2%)
    psum x1, waiting for transfers between devices, per_device(): lax.psum((grad_left, grad_right, grad_gating, grad_output, grad_norms), (...  130 us
    psum x1, waiting for transfers between devices, broadcast(): return lax.psum(block, axis)  63.4 us
    all_gather x1, waiting for transfers between devices, per_device(): row_panel = lax.all_gather(normed, 'col', axis=1, tiled=True)  47 us
    unnamed x6, waiting for transfers between devices  41.2 us
    psum x1, blocking collectives, per_device(): lax.psum((grad_left, grad_right, grad_gating, grad_output, grad_norms), (...  37.2 us
    all_to_all x1, waiting for transfers between devices, per_device(): lax.all_to_all(slab, 'col', split_axis=2, concat_axis=0, tiled=True)  23.9 us
    all_to_all x1, waiting for transfers between devices, per_device(): lax.all_to_all(spread, 'row', split_axis=0, concat_axis=0, tiled=True)  11.9 us
    convert_element_type x2, local copies, waits for them, and re-layouts, gating(): (pad_mask * sigmoid_val * values).astype(jnp.bfloat16)  11.4 us
  transfers between devices with their start and end apart: 7, of which 6 were waited for; matrix products, arithmetic and copies ran while one was open for 8% of the time, Pallas kernels for 0%

commit v1 on v0

--- a/solution.py
+++ b/solution.py
@@ -153,7 +153,9 @@
             jnp.sum(tnorm_grad, axis=(0, 1)),
         ]
     )
-    totals = lax.psum((grad_left, grad_right, grad_gating, grad_output, grad_norms), ("row", "col"))
+    totals = (grad_left, grad_right, grad_gating, grad_output, grad_norms)
+    for mesh_axis in ("col", "row"):
+        totals = lax.psum(totals, mesh_axis)
     inverse = 1.0 / tokens
     return (
         update,

time: 475 us -> 419 us (0.88)
  waiting for transfers between devices: 317 us -> 276 us
  blocking collectives: 37.2 us -> 22 us
    psum x1 -> x2, waiting for transfers between devices: 130 us -> 88.9 us  [per_device(): totals = lax.psum(totals, mesh_axis)]
    psum x1 -> x2, blocking collectives: 37.2 us -> 22 us  [per_device(): totals = lax.psum(totals, mesh_axis)]
    unnamed x6 -> x7, waiting for transfers between devices: 41.2 us -> 41.2 us
  transfers between devices with their start and end apart: 7 -> 8, of which waited for: 6 -> 7; matrix products, arithmetic and copies ran while one was open for 8% -> 10% of each run, Pallas kernels for 0% -> 0%
where the time goes in v1:
time: 419 us; the launch traced here: 418 us
  waiting for transfers between devices  276 us (66%)
  matrix products  32.8 us (8%)
  other arithmetic  32.6 us (8%)
  local copies, waits for them, and re-layouts  29.7 us (7%)
  blocking collectives  22 us (5%)
  between operations  15.1 us (4%)
  starting transfers between devices  9.47 us (2%)
    psum x2, waiting for transfers between devices, per_device(): totals = lax.psum(totals, mesh_axis)  88.9 us
    psum x1, waiting for transfers between devices, broadcast(): return lax.psum(block, axis)  63.4 us
    all_gather x1, waiting for transfers between devices, per_device(): row_panel = lax.all_gather(normed, 'col', axis=1, tiled=True)  47 us
    unnamed x7, waiting for transfers between devices  41.2 us
    all_to_all x1, waiting for transfers between devices, per_device(): lax.all_to_all(slab, 'col', split_axis=2, concat_axis=0, tiled=True)  23.9 us
    psum x2, blocking collectives, per_device(): totals = lax.psum(totals, mesh_axis)  22 us
    all_to_all x1, waiting for transfers between devices, per_device(): lax.all_to_all(spread, 'row', split_axis=0, concat_axis=0, tiled=True)  11.9 us
    convert_element_type x2, local copies, waits for them, and re-layouts, gating(): (pad_mask * sigmoid_val * values).astype(jnp.bfloat16)  11.4 us
  transfers between devices with their start and end apart: 8, of which 7 were waited for; matrix products, arithmetic and copies ran while one was open for 10% of the time, Pallas kernels for 0%

profile of v1, /device:TPU:0, one launch (start us, length us, event | category | flops | bytes accessed | tf_op | source)
XLA Modules:
  0.0 418.1 jit_solution(16828417800669415097)
XLA Ops:
  7.2 1.4 convert_reduce_fusion
  8.6 1.7 fusion.31
  10.3 2.5 fusion.25
  12.9 1.5 fusion.17
  14.4 47.0 %all-gather.2.cloned.1.call-done = bf16[32,256,128]{2,1,0:T(8,128)(2,1)} async-done(((bf16[32,64,128]{2,1,0:T(8,128)(2,1)}), bf16[32,256,128]{2,1,0:T(8,128)(2,1)}) %all-gather.2.cloned.1.call-update) | async-done | bytes 2097168 | tf_op jit(solution)/shard_map/all_gather | solution.py:75
  61.4 3.8 broadcast_select_fusion.1
  65.2 0.2 reduce-scatter.7.cloned.1.call-start
  65.5 0.8 copy-done.6
  66.2 1.3 fusion.73
  68.3 3.1 copy.54
  71.4 0.1 and_convert_fusion.1
  71.5 0.1 and_convert_fusion
  71.5 2.8 fusion.53
  74.4 2.7 fusion.5
  77.0 4.6 %copy.52 = bf16[32,256,128]{1,0,2:T(8,128)(2,1)} copy(bf16[32,256,128]{2,1,0:T(8,128)(2,1)} %fusion.5) | data formatting | bytes 4194304 | tf_op jit(solution)/shard_map/convert_element_type | solution.py:25
  81.6 63.4 %all-reduce.11.cloned.1.call-done = (bf16[32,256,128]{2,1,0:T(8,128)(2,1)}, bf16[32,256,128]{2,1,0:T(8,128)(2,1)}) async-done(((bf16[32,256,128]{2,1,0:T(8,128)(2,1)}, bf16[32,256,128]{2,1,0:T(8,128)(2,1)}), (bf16[32,256,128]{2,1,0:T(8,128)(2,1)}, bf16[32,256,128]{2,1,0:T(8,128)(2,1)})) %all-reduce.11.cloned.1.call-update) | async-done | bytes 4194320 | tf_op jit(solution)/shard_map/psum | solution.py:11
  145.1 4.5 %fusion.10 = f32[64,256,256]{2,1,0:T(8,128)S(1)} fusion(bf16[32,256,128]{2,1,0:T(8,128)(2,1)} %get-tuple-element.22, bf16[32,256,128]{2,1,0:T(8,128)(2,1)} %get-tuple-element.23, bf16[128,256]{1,0:T(8,128)(2,1)S(1)} %copy-done), kind=kOutput, calls=%fused_computation.14 | convolution fusion | flops 1075838976 | bytes 21037056 | tf_op jit(solution)/shard_map/ikc,ch->ikh/dot_general | solution.py:21
  149.6 4.3 %fusion = bf16[64,256,128]{2,1,0:T(8,128)(2,1)} fusion(f32[64,256,256]{2,1,0:T(8,128)S(1)} %fusion.10, f32[64,256]{1,0:T(8,128)S(1)} %and_convert_fusion), kind=kLoop, calls=%fused_computation.1 | loop fusion | flops 12582912 | bytes 21037056 | tf_op jit(solution)/shard_map/convert_element_type | solution.py:25
  154.0 6.8 %copy.51 = bf16[64,256,128]{1,0,2:T(8,128)(2,1)} copy(bf16[64,256,128]{2,1,0:T(8,128)(2,1)} %fusion) | data formatting | bytes 8388608 | tf_op jit(solution)/shard_map/convert_element_type | solution.py:25
  160.7 4.1 bitcast_reduce_fusion
  164.9 0.3 multiply_reduce_fusion.2
  165.2 0.3 copy-done.14
  165.5 1.3 multiply_reduce_fusion
  166.8 1.8 multiply_convert_fusion
  168.6 1.3 fusion.74
  169.9 2.2 copy.66
  172.2 0.3 reduce-scatter.5.cloned.1.call-start
  172.5 0.9 copy-done.4
  173.4 4.3 %fusion.75 = bf16[128,256,32]{1,2,0:T(8,128)(2,1)} fusion(bf16[32,64,128]{1,0,2:T(8,128)(2,1)S(1)} %copy-done.4, bf16[64,256,128]{1,0,2:T(8,128)(2,1)} %copy.51), kind=kOutput, calls=%fused_computation.136 | convolution fusion | flops 134217728 | bytes 6815744 | tf_op jit(solution)/shard_map/ijh,jkh->ikh/dot_general | solution.py:111
  177.7 4.6 %copy.56 = bf16[128,256,32]{0,1,2:T(8,128)(2,1)} copy(bf16[128,256,32]{1,2,0:T(8,128)(2,1)} %fusion.75) | data formatting | bytes 4194304 | tf_op jit(solution)/shard_map/ijh,jkh->ikh/dot_general | solution.py:111
  182.4 0.1 mul.265
  182.5 41.1 %reduce-scatter.7.cloned.1.call-done = bf16[8,32768]{1,0:T(8,128)(2,1)} async-done(((bf16[64,32768]{1,0:T(8,128)(2,1)}), bf16[8,32768]{1,0:T(8,128)(2,1)}) %reduce-scatter.7.cloned.1.call-update) | async-done | bytes 524304
  223.6 1.2 copy.71
  224.8 0.3 copy.72
  225.1 1.3 copy.58
  226.4 4.6 %all-to-all-start = ((bf16[1,8,256,128]{3,1,0,2:T(8,128)(2,1)}), bf16[1,8,256,128]{3,1,0,2:T(8,128)(2,1)}, u32[]{:S(2)}, u32[]{:S(2)}) async-start(bf16[1,8,256,128]{3,1,0,2:T(8,128)(2,1)} %copy.58), calls=%async_computation.1 | async-start | bytes 1048576 | tf_op jit(solution)/shard_map/all_to_all | solution.py:122
  231.1 1.8 fusion.51
  232.9 1.7 fusion.56
  234.6 1.1 copy.53
  235.7 23.9 %all-to-all-done = bf16[1,8,256,128]{3,1,0,2:T(8,128)(2,1)} async-done(((bf16[1,8,256,128]{3,1,0,2:T(8,128)(2,1)}), bf16[1,8,256,128]{3,1,0,2:T(8,128)(2,1)}, u32[]{:S(2)}, u32[]{:S(2)}) %all-to-all-start) | async-done | bytes 524320 | tf_op jit(solution)/shard_map/all_to_all | solution.py:122
  259.6 1.2 copy.60
  260.8 1.1 bitcast_multiply_fusion
  261.9 4.2 %all-to-all-start.1 = ((bf16[8,8,64,128]{3,2,1,0:T(8,128)(2,1)}), bf16[8,8,64,128]{3,2,1,0:T(8,128)(2,1)}, u32[]{:S(2)}, u32[]{:S(2)}) async-start(bf16[8,8,64,128]{3,2,1,0:T(8,128)(2,1)} %bitcast_multiply_fusion), calls=%async_computation.2 | async-start | bytes 2097152 | tf_op jit(solution)/shard_map/all_to_all | solution.py:127
  266.2 1.2 fusion.34
  267.4 1.0 convolution_bitcast_fusion.3
  268.4 1.0 convolution_bitcast_fusion.2
  269.4 0.3 fusion.63
  269.7 11.9 %all-to-all-done.1 = bf16[8,8,64,128]{3,2,1,0:T(8,128)(2,1)} async-done(((bf16[8,8,64,128]{3,2,1,0:T(8,128)(2,1)}), bf16[8,8,64,128]{3,2,1,0:T(8,128)(2,1)}, u32[]{:S(2)}, u32[]{:S(2)}) %all-to-all-start.1) | async-done | bytes 1048608 | tf_op jit(solution)/shard_map/all_to_all | solution.py:127
  281.5 1.1 constant_dynamic-slice_fusion
  282.7 2.8 fusion.49
  285.5 1.0 convolution_bitcast_fusion.1
  286.5 1.4 convolution_add_fusion.1
  287.9 1.0 convolution_bitcast_fusion
  289.0 2.6 fusion.30
  291.6 10.3 %psum.94 = f32[4,128]{1,0:T(4,128)S(1)} all-reduce(f32[4,128]{1,0:T(4,128)S(1)} %pad_maximum_fusion.6), channel_id=1, replica_groups=mesh['row'=8,'col'=4] {'col'}, use_global_device_ids=true, to_apply=%region_24.25 | all-reduce | flops 512 | bytes 4096 | tf_op jit(solution)/shard_map/psum | solution.py:158
  301.8 11.8 %psum.95 = f32[4,128]{1,0:T(4,128)S(1)} all-reduce(f32[4,128]{1,0:T(4,128)S(1)} %psum.94), channel_id=1, replica_groups=mesh['row'=8,'col'=4] {'row'}, use_global_device_ids=true, to_apply=%region_25.26 | all-reduce | flops 512 | bytes 4096 | tf_op jit(solution)/shard_map/psum | solution.py:158
  313.7 2.0 fusion.29
  315.7 31.4 %all-reduce.9.cloned.1.call-done = (f32[128,256]{1,0:T(8,128)}, f32[128,256]{1,0:T(8,128)}, f32[128,128]{1,0:T(8,128)}, f32[128,128]{1,0:T(8,128)}) async-done(((f32[128,256]{1,0:T(8,128)}, f32[128,256]{1,0:T(8,128)}, f32[128,128]{1,0:T(8,128)}, f32[128,128]{1,0:T(8,128)}), (f32[128,256]{1,0:T(8,128)}, f32[128,256]{1,0:T(8,128)}, f32[128,128]{1,0:T(8,128)}, ...) | async-done | bytes 393232 | tf_op jit(solution)/shard_map/psum | solution.py:158
  347.1 0.6 broadcast_multiply_fusion.10
  347.6 57.5 %all-reduce.7.cloned.1.call-done = (f32[128,256]{1,0:T(8,128)}, f32[128,256]{1,0:T(8,128)}, f32[128,128]{1,0:T(8,128)}, f32[128,128]{1,0:T(8,128)}) async-done(((f32[128,256]{1,0:T(8,128)}, f32[128,256]{1,0:T(8,128)}, f32[128,128]{1,0:T(8,128)}, f32[128,128]{1,0:T(8,128)}), (f32[128,256]{1,0:T(8,128)}, f32[128,256]{1,0:T(8,128)}, f32[128,128]{1,0:T(8,128)}, ...) | async-done | bytes 393232 | tf_op jit(solution)/shard_map/psum | solution.py:158
  405.1 1.6 broadcast_multiply_fusion
  406.7 1.6 broadcast_multiply_fusion.1
  408.3 1.5 broadcast_multiply_fusion.2
  409.7 1.5 broadcast_multiply_fusion.3
  (54 shorter events, 0.5 us)
Async XLA Ops:
  7.2 137.9 %copy-start = (bf16[128,256]{1,0:T(8,128)(2,1)S(1)}, bf16[128,256]{1,0:T(8,128)(2,1)}, u32[]{:S(2)}) copy-start(bf16[128,256]{1,0:T(8,128)(2,1)} %param.17) | copy-start | bytes 196612
  7.2 5.7 %copy-start.12 = (bf16[128,128]{1,0:T(8,128)(2,1)S(1)}, bf16[128,128]{1,0:T(8,128)(2,1)}, u32[]{:S(2)}) copy-start(bf16[128,128]{1,0:T(8,128)(2,1)} %param.18) | copy-start | bytes 98308
  7.2 54.2 %all-gather.2.cloned.1.call-start = ((), (), s32[]{:S(2)}) async-start(), calls=%async_computation.4 | async-start | bytes 2621440 | tf_op jit(solution)/shard_map/all_gather | solution.py:75
  12.8 132.2 %all-reduce.11.cloned.1.call-start = ((), (), s32[]{:S(2)}) async-start(), calls=%async_computation.9 | async-start | bytes 8388608 | tf_op jit(solution)/shard_map/psum | solution.py:11
  65.2 1.0 copy-start.6
  65.2 1.0 copy-start.11
  65.2 158.4 %reduce-scatter.7.cloned.1.call-start = ((), (), s32[]{:S(2)}) async-start(), calls=%async_computation.6 | async-start | bytes 4718592
  67.6 4.0 copy-start.9
  164.8 0.7 copy-start.14
  165.5 1.3 copy-start.15
  166.8 1.8 copy-start.1
  168.6 1.3 copy-start.3
  172.2 1.2 copy-start.4
  172.2 110.4 %reduce-scatter.5.cloned.1.call-start = ((), (), s32[]{:S(2)}) async-start(), calls=%async_computation.5 | async-start | bytes 2621440 | tf_op jit(solution)/shard_map/reduce_scatter | solution.py:115
  223.6 7.5 %copy-start.2 = (bf16[32,64,128]{2,1,0:T(8,128)(2,1)S(1)}, bf16[32,64,128]{2,1,0:T(8,128)(2,1)}, u32[]{:S(2)}) copy-start(bf16[32,64,128]{2,1,0:T(8,128)(2,1)} %fusion.25) | copy-start | bytes 1572868
  226.4 33.2 %all-to-all-start = ((bf16[1,8,256,128]{3,1,0,2:T(8,128)(2,1)}), bf16[1,8,256,128]{3,1,0,2:T(8,128)(2,1)}, u32[]{:S(2)}, u32[]{:S(2)}) async-start(bf16[1,8,256,128]{3,1,0,2:T(8,128)(2,1)} %copy.58), calls=%async_computation.1 | async-start | bytes 1048576 | tf_op jit(solution)/shard_map/all_to_all | solution.py:122
  231.1 3.5 copy-start.8
  260.8 5.4 %copy-start.7 = (bf16[32,64,128]{2,1,0:T(8,128)(2,1)S(1)}, bf16[32,64,128]{2,1,0:T(8,128)(2,1)}, u32[]{:S(2)}) copy-start(bf16[32,64,128]{2,1,0:T(8,128)(2,1)} %param.12) | copy-start | bytes 1572868
  261.9 19.6 %all-to-all-start.1 = ((bf16[8,8,64,128]{3,2,1,0:T(8,128)(2,1)}), bf16[8,8,64,128]{3,2,1,0:T(8,128)(2,1)}, u32[]{:S(2)}, u32[]{:S(2)}) async-start(bf16[8,8,64,128]{3,2,1,0:T(8,128)(2,1)} %bitcast_multiply_fusion), calls=%async_computation.2 | async-start | bytes 2097152 | tf_op jit(solution)/shard_map/all_to_all | solution.py:127
  266.2 80.9 %all-reduce.9.cloned.1.call-start = ((), (), s32[]{:S(2)}) async-start(), calls=%async_computation.8 | async-start | bytes 786432 | tf_op jit(solution)/shard_map/psum | solution.py:158
  285.5 2.5 copy-start.10
  286.5 2.5 copy-start.5
  286.5 2.5 copy-start.13
  313.6 91.5 %all-reduce.7.cloned.1.call-start = ((), (), s32[]{:S(2)}) async-start(), calls=%async_computation.7 | async-start | bytes 786432 | tf_op jit(solution)/shard_map/psum | solution.py:158
Sparse Core Ops, SparseCore 0:
  13.0 48.3 all-gather.1
  65.4 79.6 all-reduce.10
  172.3 51.2 reduce-scatter.6
  225.7 51.5 reduce-scatter.4
  313.8 33.2 all-reduce.8
  350.3 54.7 all-reduce.6
